TPU v7x, 256 devices: a whole 4x4x8 slice. The times are simulated.
256 devices in a mesh: pipe: 8 (over x, z_hi), expert: 32 (over y, z_lo, core).
Axes of the slice: x: 4, y: 4, z: 8 (z_hi: 2, z_lo: 4; z = z_hi * 4 + z_lo), core: 2. Of those that a mesh axis runs over, the one named last changes fastest.
Arguments:
- fwd_acts: bfloat16 [8, 2048, 3584], P('pipe', 'expert'), may hold values from -6 to 6
- fwd_routes: int32 [8, 2048, 2], P('pipe', 'expert'), may hold values from 0 to 7, all different within a row; in each aligned block of 64 rows (0 to 63, 64 to 127, ..., all dimensions but the last counted through in order) at most 20 rows name the same one
- fwd_gates: float32 [8, 2048, 2], P('pipe', 'expert'), may hold values from 0.25 to 1
- back_acts: bfloat16 [8, 2048, 3584], P('pipe', 'expert'), may hold values from -6 to 6
- back_routes: int32 [8, 2048, 2], P('pipe', 'expert'), may hold values from 0 to 7, all different within a row; in each aligned block of 64 rows (0 to 63, 64 to 127, ..., all dimensions but the last counted through in order) at most 20 rows name the same one
- back_gates: float32 [8, 2048, 2], P('pipe', 'expert'), may hold values from 0.25 to 1
- back_grads: bfloat16 [8, 2048, 3584], P('pipe', 'expert'), may hold values from -0.59765625 to 0.59765625
- w_up: bfloat16 [8, 32, 3584, 256], P('pipe', 'expert'), may hold values from -0.09375 to 0.09375
- w_down: bfloat16 [8, 32, 256, 3584], P('pipe', 'expert'), may hold values from -0.1875 to 0.1875
Outputs:
- fwd_next: bfloat16 [8, 2048, 3584], P('pipe', 'expert')
- back_next: bfloat16 [8, 2048, 3584], P('pipe', 'expert')
- grad_up: float32 [8, 32, 3584, 256], P('pipe', 'expert')
- grad_down: float32 [8, 32, 256, 3584], P('pipe', 'expert')
Inputs may be any that keep to these rules, and one draw needn't show every extreme that they name: `fwd_routes`: in each aligned block of 64 rows of a section the 2 experts of a row differ, and each expert is named by at most 20 rows, by exactly 20 in some block. `back_routes`: as for fwd_routes.
All inputs are finite; a program needn't handle non-finite values.
Results may differ from a plain program's by a relative error of at most 0.005.
Values may be sent and summed in bfloat16 or wider, within the bound.
A program may use at most 192 MiB of HBM per device.

v0:
```python
import jax
import jax.numpy as jnp
from jax import lax
from jax.sharding import PartitionSpec as P

GROUP = 4
HIGH = lax.Precision.HIGHEST


def passed_along(value, axis, steps):
    count = lax.axis_size(axis)
    pairs = [(source, (source + steps) % count) for source in range(count)]
    return lax.ppermute(value, axis, pairs)


def silu_grad(value):
    sigma = jax.nn.sigmoid(value)
    return sigma * (1.0 + value * (1.0 - sigma))


def tables(routes, gates, experts, slot_cap):
    tok_rows, top_count = routes.shape
    flat = routes.reshape(tok_rows * top_count)
    onehot = (flat[:, None] == jnp.arange(experts, dtype=jnp.int32)[None, :]).astype(jnp.int32)
    before = jnp.cumsum(onehot, axis=0) - onehot
    slots = jnp.sum(before * onehot, axis=1)
    places = flat * slot_cap + slots
    columns = jnp.arange(experts * slot_cap, dtype=jnp.int32)
    hits = (
        (places[:, None] == columns[None, :])
        .astype(jnp.float32)
        .reshape(tok_rows, top_count, experts * slot_cap)
    )
    plain = jnp.sum(hits, axis=1)
    gated = jnp.sum(hits * gates[:, :, None], axis=1)
    return (plain, gated)


def gather_rows(plain, values):
    return lax.dot_general(
        plain.astype(jnp.bfloat16),
        values,
        (((0,), (0,)), ((), ())),
        preferred_element_type=jnp.float32,
    ).astype(jnp.bfloat16)


def send_rows(stacked, experts, slot_cap):
    count, _, model_width = stacked.shape
    chunks = stacked.reshape(count, experts, slot_cap, model_width)
    received = lax.all_to_all(chunks, "eg", split_axis=1, concat_axis=1, tiled=True)
    gathered = lax.all_gather(received, "em", axis=1, tiled=True)
    return gathered.reshape(count, -1, model_width)


def send_back(parts, experts, slot_cap):
    count, _, model_width = parts.shape
    arranged = parts.reshape(count, GROUP, experts * slot_cap, model_width)
    received = lax.all_to_all(arranged, "em", split_axis=1, concat_axis=1, tiled=True)
    summed = jnp.sum(received, axis=1, dtype=jnp.float32).astype(jnp.bfloat16)
    summed = summed.reshape(count, experts, slot_cap, model_width)
    back = lax.all_to_all(summed, "eg", split_axis=1, concat_axis=1, tiled=True)
    return back.reshape(count, experts * slot_cap, model_width).astype(jnp.float32)


def expert_forward(rows, up_proj, down_proj):
    pre = jnp.dot(rows, up_proj, preferred_element_type=jnp.float32)
    act = jax.nn.silu(pre).astype(jnp.bfloat16)
    return jnp.dot(act, down_proj, preferred_element_type=jnp.float32).astype(jnp.bfloat16)


def expert_backward(rows, grad_rows, up_proj, down_proj):
    pre = jnp.dot(rows, up_proj, preferred_element_type=jnp.float32)
    act = jax.nn.silu(pre).astype(jnp.bfloat16)
    dact = lax.dot_general(
        grad_rows, down_proj, (((1,), (1,)), ((), ())), preferred_element_type=jnp.float32
    )
    dpre = (dact * silu_grad(pre)).astype(jnp.bfloat16)
    dpart = lax.dot_general(
        dpre, up_proj, (((1,), (1,)), ((), ())), preferred_element_type=jnp.float32
    ).astype(jnp.bfloat16)
    grad_up = lax.dot_general(
        rows, dpre, (((0,), (0,)), ((), ())), preferred_element_type=jnp.float32
    )
    grad_down = lax.dot_general(
        act, grad_rows, (((0,), (0,)), ((), ())), preferred_element_type=jnp.float32
    )
    return (dpart, grad_up, grad_down)


def local(
    fwd_acts, fwd_routes, fwd_gates, back_acts, back_routes, back_gates, back_grads, w_up, w_down
):
    devices = lax.axis_size("eg") * lax.axis_size("em")
    experts = devices // GROUP
    tok_rows = fwd_acts.shape[1]
    top_count = fwd_routes.shape[2]
    slot_cap = GROUP * (5 * tok_rows * top_count // (4 * devices))
    up_proj = w_up[0, 0]
    down_proj = w_down[0, 0]
    fwd_input = fwd_acts[0]
    back_input = back_acts[0]
    out_grad = back_grads[0]
    plain_f, gated_f = tables(fwd_routes[0], fwd_gates[0], experts, slot_cap)
    plain_b, gated_b = tables(back_routes[0], back_gates[0], experts, slot_cap)
    buffer_f = gather_rows(plain_f, fwd_input)
    buffer_x = gather_rows(plain_b, back_input)
    buffer_g = lax.dot_general(
        gated_b, out_grad.astype(jnp.float32), (((0,), (0,)), ((), ())), precision=HIGH
    ).astype(jnp.bfloat16)
    got_f = send_rows(buffer_f[None], experts, slot_cap)
    part = expert_forward(got_f[0], up_proj, down_proj)
    summed_f = send_back(part[None], experts, slot_cap)[0]
    got_b = send_rows(jnp.stack([buffer_x, buffer_g]), experts, slot_cap)
    dpart, grad_up, grad_down = expert_backward(got_b[0], got_b[1], up_proj, down_proj)
    summed_b = send_back(dpart[None], experts, slot_cap)[0]
    merged = jnp.dot(gated_f, summed_f, precision=HIGH)
    section_out = (fwd_input.astype(jnp.float32) + merged).astype(jnp.bfloat16)
    spread_back = jnp.dot(plain_b, summed_b, precision=HIGH)
    section_grad = (out_grad.astype(jnp.float32) + spread_back).astype(jnp.bfloat16)
    fwd_next = passed_along(section_out[None], "pipe", 1)
    back_next = passed_along(section_grad[None], "pipe", -1)
    return (fwd_next, back_next, grad_up[None, None], grad_down[None, None])


def solution(mesh):
    groups = mesh.shape["expert"] // GROUP
    devices = mesh.devices.reshape(mesh.shape["pipe"], groups, GROUP)
    mesh = jax.sharding.Mesh(devices, ("pipe", "eg", "em"))
    in_specs = (
        P("pipe", ("eg", "em"), None),
        P("pipe", ("eg", "em"), None),
        P("pipe", ("eg", "em"), None),
        P("pipe", ("eg", "em"), None),
        P("pipe", ("eg", "em"), None),
        P("pipe", ("eg", "em"), None),
        P("pipe", ("eg", "em"), None),
        P("pipe", ("eg", "em"), None, None),
        P("pipe", ("eg", "em"), None, None),
    )
    out_specs = (
        P("pipe", ("eg", "em"), None),
        P("pipe", ("eg", "em"), None),
        P("pipe", ("eg", "em"), None, None),
        P("pipe", ("eg", "em"), None, None),
    )
    return jax.shard_map(local, mesh=mesh, in_specs=in_specs, out_specs=out_specs, check_vma=False)
```

profile of v0, /device:TPU:1, one launch (start us, length us, event | category | flops | bytes accessed | tf_op | source)
XLA Modules:
  0.0 540.3 jit_solution(244298509199671782)
XLA Ops:
  11.0 2.5 convolution_convert_fusion.4
  14.9 41.2 %all_to_all.30 = bf16[1,8,20,3584]{3,2,0,1:T(8,128)(2,1)S(1)} all-to-all(bf16[1,8,20,3584]{3,2,0,1:T(8,128)(2,1)S(1)} %bitcast.73), channel_id=1, replica_groups=mesh['pipe'=8,'eg'=8,'em'=4] {'eg'}, dimensions={1} | all-to-all | bytes 2293760 | tf_op jit(solution)/shard_map/all_to_all | solution.py:51
  62.0 3.1 convolution_convert_fusion.2
  65.1 2.3 stack.10
  69.1 2.4 copy.70
  71.4 52.3 %all_to_all.31 = bf16[2,8,20,3584]{3,0,2,1:T(2,128)(2,1)} all-to-all(bf16[2,8,20,3584]{3,0,2,1:T(2,128)(2,1)S(1)} %copy.70), channel_id=1, replica_groups=mesh['pipe'=8,'eg'=8,'em'=4] {'eg'}, dimensions={1} | all-to-all | bytes 4587520 | tf_op jit(solution)/shard_map/all_to_all | solution.py:51
  123.7 12.2 %all-gather.3.cloned.1.call-done = bf16[1,32,20,3584]{3,1,2,0:T(8,128)(2,1)} async-done(((bf16[1,8,20,3584]{3,1,2,0:T(8,128)(2,1)}), bf16[1,32,20,3584]{3,1,2,0:T(8,128)(2,1)}) %all-gather.3.cloned.1.call-update) | async-done | bytes 4587536 | tf_op jit(solution)/shard_map/all_gather | solution.py:52
  135.9 7.3 %copy.65 = bf16[1,32,20,3584]{3,2,1,0:T(8,128)(2,1)} copy(bf16[1,32,20,3584]{3,1,2,0:T(8,128)(2,1)} %all-gather.3.cloned.1.call-done) | data formatting | bytes 9175040 | tf_op jit(solution)/shard_map/all_gather | solution.py:52
  143.2 7.4 %squeeze_reshape.3 = bf16[640,3584]{1,0:T(8,128)(2,1)} reshape(bf16[1,32,20,3584]{3,2,1,0:T(8,128)(2,1)} %copy.65) | data formatting | bytes 9175040 | tf_op jit(solution)/shard_map/squeeze;reshape | solution.py:112
  150.6 10.6 %convolution_convert_fusion.1 = bf16[640,3584]{1,0:T(8,128)(2,1)} fusion(bf16[1,1,256,3584]{3,2,1,0:T(8,128)(2,1)} %param.17, bf16[640,3584]{1,0:T(8,128)(2,1)} %squeeze_reshape.3, bf16[1,1,3584,256]{3,2,1,0:T(8,128)(2,1)S(1)} %copy-done), kind=kOutput, calls=%fused_computation.3 | convolution fusion | flops 2351923200 | bytes 12845056 | tf_op jit(solution)/shard_map/dot_general | solution.py:69
  161.2 5.2 all-to-all-start.1
  166.5 111.3 %all-gather.5.cloned.1.call-done = bf16[2,32,20,3584]{3,0,2,1:T(2,128)(2,1)} async-done(((bf16[2,8,20,3584]{3,0,2,1:T(2,128)(2,1)}), bf16[2,32,20,3584]{3,0,2,1:T(2,128)(2,1)}) %all-gather.5.cloned.1.call-update) | async-done | bytes 9175056 | tf_op jit(solution)/shard_map/all_gather | solution.py:52
  277.7 45.6 %slice_reduce_fusion = (bf16[32,20,3584]{2,1,0:T(8,128)(2,1)}, bf16[32,20,3584]{2,1,0:T(8,128)(2,1)}) fusion(bf16[2,32,20,3584]{3,0,2,1:T(2,128)(2,1)} %all-gather.5.cloned.1.call-done), kind=kLoop, calls=%fused_computation | loop fusion | bytes 18350080 | tf_op jit(solution)/shard_map/slice | solution.py:115
  323.3 7.3 %squeeze.34 = bf16[640,3584]{1,0:T(8,128)(2,1)} reshape(bf16[32,20,3584]{2,1,0:T(8,128)(2,1)} %get-tuple-element.4) | data formatting | bytes 9175040 | tf_op jit(solution)/shard_map/squeeze | solution.py:115
  330.6 7.3 %squeeze.33 = bf16[640,3584]{1,0:T(8,128)(2,1)} reshape(bf16[32,20,3584]{2,1,0:T(8,128)(2,1)} %get-tuple-element.5) | data formatting | bytes 9175040 | tf_op jit(solution)/shard_map/squeeze | solution.py:115
  337.9 3.8 fusion.8
  343.9 3.6 convolution_convert_fusion
  347.5 4.9 all-to-all-start.4
  352.4 3.1 reduce_sum.86
  356.7 46.2 %all-to-all-done.4 = bf16[1,4,160,3584]{3,2,0,1:T(8,128)(2,1)} async-done(((bf16[1,4,160,3584]{3,2,0,1:T(8,128)(2,1)}), bf16[1,4,160,3584]{3,2,0,1:T(8,128)(2,1)}, u32[]{:S(2)}, u32[]{:S(2)}) %all-to-all-start.4) | async-done | bytes 4587552 | tf_op jit(solution)/shard_map/all_to_all | solution.py:59
  402.9 6.0 %all-to-all-start.2 = ((bf16[1,8,20,3584]{3,2,0,1:T(8,128)(2,1)}), bf16[1,8,20,3584]{3,2,0,1:T(8,128)(2,1)S(1)}, u32[]{:S(2)}, u32[]{:S(2)}) async-start(bf16[1,8,20,3584]{3,2,0,1:T(8,128)(2,1)} %bitcast.72), calls=%async_computation.2 | async-start | bytes 2752512 | tf_op jit(solution)/shard_map/all_to_all | solution.py:62
  408.9 4.3 reduce_sum.91
  413.2 2.3 reshape.77
  415.4 28.6 %all-to-all-done.2 = bf16[1,8,20,3584]{3,2,0,1:T(8,128)(2,1)S(1)} async-done(((bf16[1,8,20,3584]{3,2,0,1:T(8,128)(2,1)}), bf16[1,8,20,3584]{3,2,0,1:T(8,128)(2,1)S(1)}, u32[]{:S(2)}, u32[]{:S(2)}) %all-to-all-start.2) | async-done | bytes 1146912 | tf_op jit(solution)/shard_map/all_to_all | solution.py:62
  445.1 3.6 all-to-all-start.5
  450.9 2.8 fusion.3
  453.7 3.6 collective-permute-start
  457.3 5.8 %convolution_bitcast_fusion.1 = f32[1,1,3584,256]{3,2,1,0:T(8,128)} fusion(bf16[640,3584]{1,0:T(8,128)(2,1)} %squeeze.34, bf16[640,256]{1,0:T(8,128)(2,1)S(1)} %fusion.15), kind=kOutput, calls=%fused_computation.5 | convolution fusion | flops 1174405120 | bytes 8585216 | tf_op jit(solution)/shard_map/dot_general | solution.py:82
  463.1 38.9 %all-to-all-done.5 = bf16[1,8,20,3584]{3,2,0,1:T(8,128)(2,1)S(1)} async-done(((bf16[1,8,20,3584]{3,2,0,1:T(8,128)(2,1)}), bf16[1,8,20,3584]{3,2,0,1:T(8,128)(2,1)S(1)}, u32[]{:S(2)}, u32[]{:S(2)}) %all-to-all-start.5) | async-done | bytes 1146912 | tf_op jit(solution)/shard_map/all_to_all | solution.py:62
  505.1 4.8 collective-permute-start.1
  510.0 5.8 %convolution_bitcast_fusion = f32[1,1,256,3584]{3,2,1,0:T(8,128)} fusion(bf16[640,3584]{1,0:T(8,128)(2,1)} %squeeze.33, f32[640,256]{1,0:T(8,128)S(1)} %copy-done.4), kind=kOutput, calls=%fused_computation.4 | convolution fusion | flops 1175224320 | bytes 8912896 | tf_op jit(solution)/shard_map/dot_general | solution.py:85
  515.7 15.2 %collective-permute-done.1 = bf16[1,64,3584]{2,1,0:T(8,128)(2,1)S(1)} collective-permute-done((bf16[1,64,3584]{2,1,0:T(8,128)(2,1)S(1)}, bf16[1,64,3584]{2,1,0:T(8,128)(2,1)S(1)}, u32[]{:S(2)}, u32[]{:S(2)}) %collective-permute-start.1) | collective-permute-done | bytes 458784 | tf_op jit(solution)/shard_map/ppermute | solution.py:13
  (58 shorter events, 25.3 us)
Async XLA Ops:
  7.2 143.4 %copy-start = (bf16[1,1,3584,256]{3,2,1,0:T(8,128)(2,1)S(1)}, bf16[1,1,3584,256]{3,2,1,0:T(8,128)(2,1)}, u32[]{:S(2)}) copy-start(bf16[1,1,3584,256]{3,2,1,0:T(8,128)(2,1)} %param.16) | copy-start | bytes 5505028
  7.2 128.7 %all-gather.3.cloned.1.call-start = ((), (), s32[]{:S(2)}) async-start(), calls=%async_computation.6 | async-start | bytes 5734400 | tf_op jit(solution)/shard_map/all_gather | solution.py:52
  56.1 1.4 copy-start.8
  56.1 2.3 copy-start.9
  56.1 3.1 copy-start.7
  57.5 220.3 %all-gather.5.cloned.1.call-start = ((), (), s32[]{:S(2)}) async-start(), calls=%async_computation.7 | async-start | bytes 11468800 | tf_op jit(solution)/shard_map/all_gather | solution.py:52
  58.5 0.6 copy-start.5
  161.2 186.3 %all-to-all-start.1 = ((bf16[1,4,160,3584]{3,2,0,1:T(8,128)(2,1)}), bf16[1,4,160,3584]{3,2,0,1:T(8,128)(2,1)}, u32[]{:S(2)}, u32[]{:S(2)}) async-start(bf16[1,4,160,3584]{3,2,0,1:T(8,128)(2,1)} %bitcast.74), calls=%async_computation.1 | async-start | bytes 9175040 | tf_op jit(solution)/shard_map/all_to_all | solution.py:59
  337.9 4.7 copy-start.1
  337.9 4.7 copy-start.10
  341.7 0.9 copy-start.3
  347.5 55.4 %all-to-all-start.4 = ((bf16[1,4,160,3584]{3,2,0,1:T(8,128)(2,1)}), bf16[1,4,160,3584]{3,2,0,1:T(8,128)(2,1)}, u32[]{:S(2)}, u32[]{:S(2)}) async-start(bf16[1,4,160,3584]{3,2,0,1:T(8,128)(2,1)} %bitcast.71), calls=%async_computation.4 | async-start | bytes 9175040 | tf_op jit(solution)/shard_map/all_to_all | solution.py:59
  402.9 41.1 %all-to-all-start.2 = ((bf16[1,8,20,3584]{3,2,0,1:T(8,128)(2,1)}), bf16[1,8,20,3584]{3,2,0,1:T(8,128)(2,1)S(1)}, u32[]{:S(2)}, u32[]{:S(2)}) async-start(bf16[1,8,20,3584]{3,2,0,1:T(8,128)(2,1)} %bitcast.72), calls=%async_computation.2 | async-start | bytes 2752512 | tf_op jit(solution)/shard_map/all_to_all | solution.py:62
  444.0 1.1 copy-start.2
  445.1 56.8 %all-to-all-start.5 = ((bf16[1,8,20,3584]{3,2,0,1:T(8,128)(2,1)}), bf16[1,8,20,3584]{3,2,0,1:T(8,128)(2,1)S(1)}, u32[]{:S(2)}, u32[]{:S(2)}) async-start(bf16[1,8,20,3584]{3,2,0,1:T(8,128)(2,1)} %bitcast.16), calls=%async_computation.5 | async-start | bytes 2752512 | tf_op jit(solution)/shard_map/all_to_all | solution.py:62
  453.7 62.1 %collective-permute-start = (bf16[1,64,3584]{2,1,0:T(8,128)(2,1)}, bf16[1,64,3584]{2,1,0:T(8,128)(2,1)}, u32[]{:S(2)}, u32[]{:S(2)}) collective-permute-start(bf16[1,64,3584]{2,1,0:T(8,128)(2,1)} %fusion.3), channel_id=1, source_target_pairs={{0,32},{32,64},{64,96},{96,128},{128,160},{160,192},{192,224},{224... | collective-permute-start | bytes 1376264 | tf_op jit(solution)/shard_map/ppermute | solution.py:13
  463.1 40.0 %copy-start.6 = (f32[64,160]{1,0:T(8,128)S(1)}, f32[64,160]{1,0:T(8,128)}, u32[]{:S(2)}) copy-start(f32[64,160]{1,0:T(8,128)} %copy-done.5) | copy-start | bytes 122884
  503.1 6.9 %copy-start.4 = (f32[640,256]{1,0:T(8,128)S(1)}, f32[640,256]{1,0:T(8,128)}, u32[]{:S(2)}) copy-start(f32[640,256]{1,0:T(8,128)} %copy-done.3) | copy-start | bytes 1966084
  505.1 25.8 %collective-permute-start.1 = (bf16[1,64,3584]{2,1,0:T(8,128)(2,1)S(1)}, bf16[1,64,3584]{2,1,0:T(8,128)(2,1)S(1)}, u32[]{:S(2)}, u32[]{:S(2)}) collective-permute-start(bf16[1,64,3584]{2,1,0:T(8,128)(2,1)S(1)} %fusion.2), channel_id=1, source_target_pairs={{0,224},{32,0},{64,32},{96,64},{128,96},{160,128},{192,160},{224,1... | collective-permute-start | bytes 1376264 | tf_op jit(solution)/shard_map/ppermute | solution.py:13
Sparse Core Ops, SparseCore 0:
  57.6 78.2 all-gather.2
  137.7 140.0 all-gather.4
where the time goes:
time: 542 us; the launch traced here: 540 us
  waiting for transfers between devices  252 us (46%)
  local copies, waits for them, and re-layouts  97.2 us (18%)
  blocking collectives  93.4 us (17%)
  matrix products  42.9 us (8%)
  starting transfers between devices  28.2 us (5%)
  between operations  14.2 us (3%)
  other arithmetic  12.1 us (2%)
    all_gather x2, waiting for transfers between devices, send_rows(): gathered = lax.all_gather(received, 'em', axis=1, tiled=True)  123 us
    all_to_all x2, blocking collectives, send_rows(): lax.all_to_all(chunks, 'eg', split_axis=1, concat_axis=1, tiled=True)  93.4 us
    all_to_all x2, waiting for transfers between devices, send_back(): back = lax.all_to_all(summed, 'eg', split_axis=1, concat_axis=1, tiled=True)  67.4 us
    all_to_all x2, waiting for transfers between devices, send_back(): lax.all_to_all(arranged, 'em', split_axis=1, concat_axis=1, tiled=True)  46.2 us
    slice x1, local copies, waits for them, and re-layouts, local(): got_b[0]  45.6 us
    ppermute x2, waiting for transfers between devices, passed_along(): return lax.ppermute(value, axis, pairs)  15.2 us
  transfers between devices with their start and end apart: 8, of which 6 were waited for; matrix products, arithmetic and copies ran while one was open for 26% of the time, Pallas kernels for 0%

commit v1 on v0

--- a/solution.py
+++ b/solution.py
@@ -48,7 +48,10 @@
 def send_rows(stacked, experts, slot_cap):
     count, _, model_width = stacked.shape
     chunks = stacked.reshape(count, experts, slot_cap, model_width)
-    received = lax.all_to_all(chunks, "eg", split_axis=1, concat_axis=1, tiled=True)
+    received = jnp.concatenate(
+        lax.all_to_all(jnp.stack(jnp.split(chunks, lax.axis_size("eg"), axis=1)), "eg", 0, 0),
+        axis=1,
+    )
     gathered = lax.all_gather(received, "em", axis=1, tiled=True)
     return gathered.reshape(count, -1, model_width)
 

time: 542 us -> 548 us (1.011)
  blocking collectives: 93.4 us -> 55.2 us
  local copies, waits for them, and re-layouts: 97.2 us -> 124 us
  waiting for transfers between devices: 252 us -> 264 us
  starting transfers between devices: 28.2 us -> 36 us
    all_to_all x2 -> x1, blocking collectives: 93.4 us -> 55.2 us  [send_rows(): lax.all_to_all(jnp.stack(jnp.split(chunks, lax.axis_size('eg'), axis=1)),...]
    unnamed x26 -> x41, local copies, waits for them, and re-layouts: 6.15 us -> 25.6 us
    all_to_all x0 -> x1, waiting for transfers between devices: none -> 11.1 us  [send_rows(): lax.all_to_all(jnp.stack(jnp.split(chunks, lax.axis_size('eg'), axis=1)),...]
    all_to_all x0 -> x1, starting transfers between devices: none -> 7.73 us  [send_rows(): lax.all_to_all(jnp.stack(jnp.split(chunks, lax.axis_size('eg'), axis=1)),...]
    another operation x0 -> x3, local copies, waits for them, and re-layouts: none -> 5.95 us  [send_rows(): jnp.stack(jnp.split(chunks, lax.axis_size('eg'), axis=1))]
  transfers between devices with their start and end apart: 8 -> 9, of which waited for: 6 -> 7; matrix products, arithmetic and copies ran while one was open for 26% -> 29% of each run, Pallas kernels for 0% -> 0%
where the time goes in v1:
time: 548 us; the launch traced here: 546 us
  waiting for transfers between devices  264 us (48%)
  local copies, waits for them, and re-layouts  124 us (23%)
  blocking collectives  55.2 us (10%)
  matrix products  42.9 us (8%)
  starting transfers between devices  36 us (7%)
  between operations  14.2 us (3%)
  other arithmetic  10.5 us (2%)
    all_gather x2, waiting for transfers between devices, send_rows(): gathered = lax.all_gather(received, 'em', axis=1, tiled=True)  124 us
    all_to_all x2, waiting for transfers between devices, send_back(): back = lax.all_to_all(summed, 'eg', split_axis=1, concat_axis=1, tiled=True)  67.4 us
    all_to_all x1, blocking collectives, send_rows(): lax.all_to_all(jnp.stack(jnp.split(chunks, lax.axis_size('eg'), axis=1)),...  55.2 us
    all_to_all x2, waiting for transfers between devices, send_back(): lax.all_to_all(arranged, 'em', split_axis=1, concat_axis=1, tiled=True)  46.2 us
    slice x1, local copies, waits for them, and re-layouts, local(): got_b[0]  45.6 us
    unnamed x41, local copies, waits for them, and re-layouts  25.6 us
    ppermute x2, waiting for transfers between devices, passed_along(): return lax.ppermute(value, axis, pairs)  15.2 us
    all_to_all x1, waiting for transfers between devices, send_rows(): lax.all_to_all(jnp.stack(jnp.split(chunks, lax.axis_size('eg'), axis=1)),...  11.1 us
  transfers between devices with their start and end apart: 9, of which 7 were waited for; matrix products, arithmetic and copies ran while one was open for 29% of the time, Pallas kernels for 0%

profile of v1, /device:TPU:1, one launch (start us, length us, event | category | flops | bytes accessed | tf_op | source)
XLA Modules:
  0.0 546.0 jit_solution(216900043006331128)
XLA Ops:
  11.0 2.5 convolution_convert_fusion.4
  20.3 7.7 %all-to-all-start = ((bf16[8,1,1,20,3584]{4,3,2,1,0:T(8,128)(2,1)}), bf16[8,1,1,20,3584]{4,3,2,1,0:T(8,128)(2,1)S(1)}, u32[]{:S(2)}, u32[]{:S(2)}) async-start(bf16[8,1,1,20,3584]{4,3,2,1,0:T(8,128)(2,1)} %fusion.35), calls=%async_computation | async-start | bytes 2752512 | tf_op jit(solution)/shard_map/all_to_all | solution.py:52
  34.5 2.6 constant_dynamic-update-slice_fusion.1
  41.4 2.5 constant_dynamic-update-slice_fusion
  50.9 11.1 %all-to-all-done = bf16[8,1,1,20,3584]{4,3,2,1,0:T(8,128)(2,1)S(1)} async-done(((bf16[8,1,1,20,3584]{4,3,2,1,0:T(8,128)(2,1)}), bf16[8,1,1,20,3584]{4,3,2,1,0:T(8,128)(2,1)S(1)}, u32[]{:S(2)}, u32[]{:S(2)}) %all-to-all-start) | async-done | bytes 1146912 | tf_op jit(solution)/shard_map/all_to_all | solution.py:52
  70.3 3.5 copy.80
  73.9 55.2 %all_to_all.30 = bf16[8,2,1,20,3584]{4,1,3,2,0:T(2,128)(2,1)} all-to-all(bf16[8,2,1,20,3584]{4,1,3,2,0:T(2,128)(2,1)S(1)} %copy.80), channel_id=1, replica_groups=mesh['pipe'=8,'eg'=8,'em'=4] {'eg'}, dimensions={0} | all-to-all | bytes 4587520 | tf_op jit(solution)/shard_map/all_to_all | solution.py:52
  129.1 12.4 %all-gather.5.cloned.1.call-done = bf16[32,1,1,20,3584]{4,0,3,2,1:T(8,128)(2,1)} async-done(((bf16[8,1,1,20,3584]{4,0,3,2,1:T(8,128)(2,1)}), bf16[32,1,1,20,3584]{4,0,3,2,1:T(8,128)(2,1)}) %all-gather.5.cloned.1.call-update) | async-done | bytes 4587536 | tf_op jit(solution)/shard_map/all_gather | solution.py:55
  141.5 7.3 %copy.68 = bf16[32,1,1,20,3584]{4,3,0,2,1:T(8,128)(2,1)} copy(bf16[32,1,1,20,3584]{4,0,3,2,1:T(8,128)(2,1)} %all-gather.5.cloned.1.call-done) | data formatting | bytes 9175040 | tf_op jit(solution)/shard_map/all_gather | solution.py:55
  148.8 7.4 %squeeze_reshape.3 = bf16[640,3584]{1,0:T(8,128)(2,1)} reshape(bf16[32,1,1,20,3584]{4,3,0,2,1:T(8,128)(2,1)} %copy.68) | data formatting | bytes 9175040 | tf_op jit(solution)/shard_map/squeeze;reshape | solution.py:115
  156.2 10.6 %convolution_convert_fusion.1 = bf16[640,3584]{1,0:T(8,128)(2,1)} fusion(bf16[1,1,256,3584]{3,2,1,0:T(8,128)(2,1)} %param.17, bf16[640,3584]{1,0:T(8,128)(2,1)} %squeeze_reshape.3, bf16[1,1,3584,256]{3,2,1,0:T(8,128)(2,1)S(1)} %copy-done), kind=kOutput, calls=%fused_computation.3 | convolution fusion | flops 2351923200 | bytes 12845056 | tf_op jit(solution)/shard_map/dot_general | solution.py:72
  166.8 5.2 all-to-all-start.1
  172.1 111.3 %all-gather.7.cloned.1.call-done = bf16[2,32,1,20,3584]{4,0,3,2,1:T(2,128)(2,1)} async-done(((bf16[2,8,1,20,3584]{4,0,3,2,1:T(2,128)(2,1)}), bf16[2,32,1,20,3584]{4,0,3,2,1:T(2,128)(2,1)}) %all-gather.7.cloned.1.call-update) | async-done | bytes 9175056 | tf_op jit(solution)/shard_map/all_gather | solution.py:55
  283.4 45.6 %slice_reduce_fusion = (bf16[32,20,3584]{2,1,0:T(8,128)(2,1)}, bf16[32,20,3584]{2,1,0:T(8,128)(2,1)}) fusion(bf16[2,32,1,20,3584]{4,0,3,2,1:T(2,128)(2,1)} %all-gather.7.cloned.1.call-done), kind=kLoop, calls=%fused_computation | loop fusion | bytes 18350080 | tf_op jit(solution)/shard_map/slice | solution.py:118
  328.9 7.3 %squeeze.34 = bf16[640,3584]{1,0:T(8,128)(2,1)} reshape(bf16[32,20,3584]{2,1,0:T(8,128)(2,1)} %get-tuple-element.4) | data formatting | bytes 9175040 | tf_op jit(solution)/shard_map/squeeze | solution.py:118
  336.2 7.3 %squeeze.33 = bf16[640,3584]{1,0:T(8,128)(2,1)} reshape(bf16[32,20,3584]{2,1,0:T(8,128)(2,1)} %get-tuple-element.5) | data formatting | bytes 9175040 | tf_op jit(solution)/shard_map/squeeze | solution.py:118
  343.5 3.8 fusion.8
  349.5 3.6 convolution_convert_fusion
  353.1 4.9 all-to-all-start.4
  358.0 3.1 reduce_sum.86
  362.3 46.2 %all-to-all-done.4 = bf16[1,4,160,3584]{3,2,0,1:T(8,128)(2,1)} async-done(((bf16[1,4,160,3584]{3,2,0,1:T(8,128)(2,1)}), bf16[1,4,160,3584]{3,2,0,1:T(8,128)(2,1)}, u32[]{:S(2)}, u32[]{:S(2)}) %all-to-all-start.4) | async-done | bytes 4587552 | tf_op jit(solution)/shard_map/all_to_all | solution.py:62
  408.5 6.0 %all-to-all-start.2 = ((bf16[1,8,20,3584]{3,2,0,1:T(8,128)(2,1)}), bf16[1,8,20,3584]{3,2,0,1:T(8,128)(2,1)S(1)}, u32[]{:S(2)}, u32[]{:S(2)}) async-start(bf16[1,8,20,3584]{3,2,0,1:T(8,128)(2,1)} %bitcast.153), calls=%async_computation.2 | async-start | bytes 2752512 | tf_op jit(solution)/shard_map/all_to_all | solution.py:65
  414.5 4.3 reduce_sum.91
  421.1 28.6 %all-to-all-done.2 = bf16[1,8,20,3584]{3,2,0,1:T(8,128)(2,1)S(1)} async-done(((bf16[1,8,20,3584]{3,2,0,1:T(8,128)(2,1)}), bf16[1,8,20,3584]{3,2,0,1:T(8,128)(2,1)S(1)}, u32[]{:S(2)}, u32[]{:S(2)}) %all-to-all-start.2) | async-done | bytes 1146912 | tf_op jit(solution)/shard_map/all_to_all | solution.py:65
  450.7 3.6 all-to-all-start.5
  456.5 2.8 fusion.3
  459.3 3.6 collective-permute-start
  462.9 5.8 %convolution_bitcast_fusion.1 = f32[1,1,3584,256]{3,2,1,0:T(8,128)} fusion(bf16[640,3584]{1,0:T(8,128)(2,1)} %squeeze.34, bf16[640,256]{1,0:T(8,128)(2,1)S(1)} %fusion.15), kind=kOutput, calls=%fused_computation.5 | convolution fusion | flops 1174405120 | bytes 8585216 | tf_op jit(solution)/shard_map/dot_general | solution.py:85
  468.7 38.9 %all-to-all-done.5 = bf16[1,8,20,3584]{3,2,0,1:T(8,128)(2,1)S(1)} async-done(((bf16[1,8,20,3584]{3,2,0,1:T(8,128)(2,1)}), bf16[1,8,20,3584]{3,2,0,1:T(8,128)(2,1)S(1)}, u32[]{:S(2)}, u32[]{:S(2)}) %all-to-all-start.5) | async-done | bytes 1146912 | tf_op jit(solution)/shard_map/all_to_all | solution.py:65
  510.7 4.8 collective-permute-start.1
  515.6 5.8 %convolution_bitcast_fusion = f32[1,1,256,3584]{3,2,1,0:T(8,128)} fusion(bf16[640,3584]{1,0:T(8,128)(2,1)} %squeeze.33, f32[640,256]{1,0:T(8,128)S(1)} %copy-done.5), kind=kOutput, calls=%fused_computation.4 | convolution fusion | flops 1175224320 | bytes 8912896 | tf_op jit(solution)/shard_map/dot_general | solution.py:88
  521.3 15.2 %collective-permute-done.1 = bf16[1,64,3584]{2,1,0:T(8,128)(2,1)S(1)} collective-permute-done((bf16[1,64,3584]{2,1,0:T(8,128)(2,1)S(1)}, bf16[1,64,3584]{2,1,0:T(8,128)(2,1)S(1)}, u32[]{:S(2)}, u32[]{:S(2)}) %collective-permute-start.1) | collective-permute-done | bytes 458784 | tf_op jit(solution)/shard_map/ppermute | solution.py:13
  (76 shorter events, 51.4 us)
Async XLA Ops:
  7.2 149.0 %copy-start = (bf16[1,1,3584,256]{3,2,1,0:T(8,128)(2,1)S(1)}, bf16[1,1,3584,256]{3,2,1,0:T(8,128)(2,1)}, u32[]{:S(2)}) copy-start(bf16[1,1,3584,256]{3,2,1,0:T(8,128)(2,1)} %param.16) | copy-start | bytes 5505028
  16.9 11.2 %copy-start.8 = (s32[1,64,2]{1,2,0:T(2,128)S(1)}, s32[1,64,2]{1,2,0:T(2,128)}, u32[]{:S(2)}) copy-start(s32[1,64,2]{1,2,0:T(2,128)} %param.13) | copy-start | bytes 1540
  17.6 11.4 %copy-start.9 = (f32[1,64,2]{1,2,0:T(2,128)S(1)}, f32[1,64,2]{1,2,0:T(2,128)}, u32[]{:S(2)}) copy-start(f32[1,64,2]{1,2,0:T(2,128)} %param.14) | copy-start | bytes 1540
  20.3 41.7 %all-to-all-start = ((bf16[8,1,1,20,3584]{4,3,2,1,0:T(8,128)(2,1)}), bf16[8,1,1,20,3584]{4,3,2,1,0:T(8,128)(2,1)S(1)}, u32[]{:S(2)}, u32[]{:S(2)}) async-start(bf16[8,1,1,20,3584]{4,3,2,1,0:T(8,128)(2,1)} %fusion.35), calls=%async_computation | async-start | bytes 2752512 | tf_op jit(solution)/shard_map/all_to_all | solution.py:52
  28.0 113.5 %all-gather.5.cloned.1.call-start = ((), (), s32[]{:S(2)}) async-start(), calls=%async_computation.6 | async-start | bytes 5734400 | tf_op jit(solution)/shard_map/all_gather | solution.py:55
  29.1 0.6 copy-start.6
  34.5 2.6 copy-start.3
  63.3 220.0 %all-gather.7.cloned.1.call-start = ((), (), s32[]{:S(2)}) async-start(), calls=%async_computation.7 | async-start | bytes 11468800 | tf_op jit(solution)/shard_map/all_gather | solution.py:55
  166.8 186.3 %all-to-all-start.1 = ((bf16[1,4,160,3584]{3,2,0,1:T(8,128)(2,1)}), bf16[1,4,160,3584]{3,2,0,1:T(8,128)(2,1)}, u32[]{:S(2)}, u32[]{:S(2)}) async-start(bf16[1,4,160,3584]{3,2,0,1:T(8,128)(2,1)} %bitcast.154), calls=%async_computation.1 | async-start | bytes 9175040 | tf_op jit(solution)/shard_map/all_to_all | solution.py:62
  343.5 4.7 copy-start.1
  343.5 4.7 copy-start.10
  347.3 0.9 copy-start.4
  353.1 55.4 %all-to-all-start.4 = ((bf16[1,4,160,3584]{3,2,0,1:T(8,128)(2,1)}), bf16[1,4,160,3584]{3,2,0,1:T(8,128)(2,1)}, u32[]{:S(2)}, u32[]{:S(2)}) async-start(bf16[1,4,160,3584]{3,2,0,1:T(8,128)(2,1)} %bitcast.151), calls=%async_computation.4 | async-start | bytes 9175040 | tf_op jit(solution)/shard_map/all_to_all | solution.py:62
  408.5 41.1 %all-to-all-start.2 = ((bf16[1,8,20,3584]{3,2,0,1:T(8,128)(2,1)}), bf16[1,8,20,3584]{3,2,0,1:T(8,128)(2,1)S(1)}, u32[]{:S(2)}, u32[]{:S(2)}) async-start(bf16[1,8,20,3584]{3,2,0,1:T(8,128)(2,1)} %bitcast.153), calls=%async_computation.2 | async-start | bytes 2752512 | tf_op jit(solution)/shard_map/all_to_all | solution.py:65
  449.6 1.1 copy-start.2
  450.7 56.8 %all-to-all-start.5 = ((bf16[1,8,20,3584]{3,2,0,1:T(8,128)(2,1)}), bf16[1,8,20,3584]{3,2,0,1:T(8,128)(2,1)S(1)}, u32[]{:S(2)}, u32[]{:S(2)}) async-start(bf16[1,8,20,3584]{3,2,0,1:T(8,128)(2,1)} %bitcast.32), calls=%async_computation.5 | async-start | bytes 2752512 | tf_op jit(solution)/shard_map/all_to_all | solution.py:65
  459.3 62.0 %collective-permute-start = (bf16[1,64,3584]{2,1,0:T(8,128)(2,1)}, bf16[1,64,3584]{2,1,0:T(8,128)(2,1)}, u32[]{:S(2)}, u32[]{:S(2)}) collective-permute-start(bf16[1,64,3584]{2,1,0:T(8,128)(2,1)} %fusion.3), channel_id=1, source_target_pairs={{0,32},{32,64},{64,96},{96,128},{128,160},{160,192},{192,224},{224... | collective-permute-start | bytes 1376264 | tf_op jit(solution)/shard_map/ppermute | solution.py:13
  468.7 40.0 %copy-start.7 = (f32[64,160]{1,0:T(8,128)S(1)}, f32[64,160]{1,0:T(8,128)}, u32[]{:S(2)}) copy-start(f32[64,160]{1,0:T(8,128)} %copy-done.6) | copy-start | bytes 122884
  508.7 6.9 %copy-start.5 = (f32[640,256]{1,0:T(8,128)S(1)}, f32[640,256]{1,0:T(8,128)}, u32[]{:S(2)}) copy-start(f32[640,256]{1,0:T(8,128)} %copy-done.4) | copy-start | bytes 1966084
  510.7 25.8 %collective-permute-start.1 = (bf16[1,64,3584]{2,1,0:T(8,128)(2,1)S(1)}, bf16[1,64,3584]{2,1,0:T(8,128)(2,1)S(1)}, u32[]{:S(2)}, u32[]{:S(2)}) collective-permute-start(bf16[1,64,3584]{2,1,0:T(8,128)(2,1)S(1)} %fusion.2), channel_id=1, source_target_pairs={{0,224},{32,0},{64,32},{96,64},{128,96},{160,128},{192,160},{224,1... | collective-permute-start | bytes 1376264 | tf_op jit(solution)/shard_map/ppermute | solution.py:13
Sparse Core Ops, SparseCore 0:
  63.5 77.9 all-gather.4
  143.3 140.0 all-gather.6
